TPU v7x, 256 devices: a whole 4x4x8 slice. The times are simulated.
256 devices in a mesh: slab: 8 (over x_lo, y), brick: 32 (over x_hi, z, core).
Axes of the slice: x: 4 (x_hi: 2, x_lo: 2; x = x_hi * 2 + x_lo), y: 4, z: 8, core: 2. Of those that a mesh axis runs over, the one named last changes fastest.
Arguments:
- embed: bfloat16 [262144, 512], P(('slab', 'brick')), may hold values from -6 to 6
- cotangent: bfloat16 [262144, 512], P(('slab', 'brick')), may hold values from -6 to 6
- basis: bfloat16 [16, 16, 262144], P(None, None, ('slab', 'brick')), may hold values from -4 to 4
- triplet_row_index: int32 [16, 262144], P(None, ('slab', 'brick')), may hold values from 0 to 1535
- triplet_slot_count: int32 [262144], P(('slab', 'brick')), may hold values from 1 to 16, as said below
- outgoing_edge_rows: int32 [4, 32768], P(None, ('slab', 'brick')), may hold values from 0 to 1023
- residual_weight: bfloat16 [512, 512], replicated, may hold values from -0.25 to 0.25
- down_weight: bfloat16 [512, 64], replicated, may hold values from -0.25 to 0.25
- up_weight: bfloat16 [64, 512], replicated, may hold values from -0.75 to 0.75
- basis_weight: bfloat16 [16, 64], replicated, may hold values from -1.5 to 1.5
Outputs:
- edge_embedding_gradient: bfloat16 [262144, 512], P(('slab', 'brick'))
- residual_weight_gradient: float32 [512, 512], replicated
- down_weight_gradient: float32 [512, 64], replicated
- up_weight_gradient: float32 [64, 512], replicated
- basis_weight_gradient: float32 [16, 64], replicated
Inputs may be any that keep to these rules, and one draw needn't show every extreme that they name: `triplet_row_index`: indices refer to the extended table of the edge's own brick. `triplet_slot_count`: slots at or past the count are empty; in every brick some edge fills all 16 slots; bricks differ in density. `outgoing_edge_rows`: local row numbers within the sending brick; a row may appear more than once.
All inputs are finite; a program needn't handle non-finite values.
Results may differ from a plain program's by a relative error of at most 0.006.
Values may be sent and summed in bfloat16 or wider, within the bound.
A program may use at most 64 MiB of HBM per device.

v0:
```python
import jax
import jax.numpy as jnp
from jax import lax
from jax.sharding import PartitionSpec as P


def passed_along(value, axis, steps):
    count = lax.axis_size(axis)
    pairs = [(source, (source + steps) % count) for source in range(count)]
    return lax.ppermute(value, axis, pairs)


def silu_grad(value):
    sig = jax.nn.sigmoid(value)
    return sig * (1.0 + value * (1.0 - sig))


def selector(index_row, count_rows, dtype):
    positions = lax.broadcasted_iota(jnp.int32, (count_rows, index_row.shape[0]), 0)
    return (positions == index_row[None, :]).astype(dtype)


def shards(
    embed,
    cotangent,
    basis,
    triplet_row_index,
    triplet_slot_count,
    outgoing_edge_rows,
    residual_weight,
    down_weight,
    up_weight,
    basis_weight,
):
    rows = embed.shape[0]
    ghost = outgoing_edge_rows.shape[1]
    trips = triplet_row_index.shape[0]
    res_pre = jnp.dot(embed, residual_weight, preferred_element_type=jnp.float32)
    dres = (cotangent.astype(jnp.float32) * silu_grad(res_pre)).astype(jnp.bfloat16)
    residual_weight_gradient = lax.dot_general(
        embed, dres, (((0,), (0,)), ((), ())), preferred_element_type=jnp.float32
    )
    res_term = lax.dot_general(
        dres, residual_weight, (((1,), (1,)), ((), ())), preferred_element_type=jnp.float32
    )
    pre = lax.dot_general(
        down_weight, embed, (((0,), (1,)), ((), ())), preferred_element_type=jnp.float32
    )
    proj = jax.nn.silu(pre).astype(jnp.bfloat16)
    picks = [selector(outgoing_edge_rows[step], rows, jnp.bfloat16) for step in range(4)]
    received = []
    for step, by in enumerate((1, -1)):
        chosen = jnp.dot(proj, picks[step], preferred_element_type=jnp.float32).astype(jnp.bfloat16)
        received.append(passed_along(chosen, "slab", by))
    for step, by in enumerate((1, -1)):
        chosen = jnp.dot(proj, picks[step + 2], preferred_element_type=jnp.float32).astype(
            jnp.bfloat16
        )
        received.append(passed_along(chosen, "brick", by))
    ghost_proj = jnp.concatenate(received, axis=1)
    edge_table_rows = jnp.concatenate([proj, ghost_proj], axis=1)
    table_rows = edge_table_rows.shape[1]
    weight_list = jnp.einsum("unz,nh->uhz", basis, basis_weight, preferred_element_type=jnp.float32)
    live = (lax.broadcasted_iota(jnp.int32, (trips, rows), 0) < triplet_slot_count[None, :]).astype(
        jnp.float32
    )

    def gather_slot(carry, index_row):
        onehot = selector(index_row, table_rows, jnp.bfloat16)
        picked = jnp.dot(edge_table_rows, onehot, preferred_element_type=jnp.float32).astype(
            jnp.bfloat16
        )
        return (carry, picked)

    _, gathered = lax.scan(gather_slot, jnp.zeros((), jnp.float32), triplet_row_index)
    gathered = gathered.astype(jnp.float32)
    tsum = jnp.sum(weight_list * gathered * live[:, None, :], axis=0)
    activation_value = jax.nn.silu(tsum).astype(jnp.bfloat16)
    dsum = lax.dot_general(
        up_weight, cotangent, (((1,), (1,)), ((), ())), preferred_element_type=jnp.float32
    )
    dt = dsum * silu_grad(tsum)
    up_weight_gradient = lax.dot_general(
        activation_value, cotangent, (((1,), (0,)), ((), ())), preferred_element_type=jnp.float32
    )
    weight_gradient_list = (dt[None, :, :] * gathered * live[:, None, :]).astype(jnp.bfloat16)
    basis_weight_gradient = jnp.einsum(
        "yqi,ywi->qw", basis, weight_gradient_list, preferred_element_type=jnp.float32
    )
    dhx = dt[None, :, :] * weight_list * live[:, None, :]

    def scatter_slot(total, inputs):
        index_row, slot_terms = inputs
        onehot = selector(index_row, table_rows, jnp.float32)
        added = lax.dot_general(
            slot_terms,
            onehot,
            (((1,), (1,)), ((), ())),
            precision=lax.Precision.HIGHEST,
            preferred_element_type=jnp.float32,
        )
        return (total + added, None)

    table_gradient, _ = lax.scan(
        scatter_slot,
        jnp.zeros((edge_table_rows.shape[0], table_rows), jnp.float32),
        (triplet_row_index, dhx),
    )
    dproj = table_gradient[:, :rows]
    for step, by in enumerate((1, -1)):
        block = table_gradient[:, rows + step * ghost : rows + (step + 1) * ghost]
        back = passed_along(block, "slab", -by)
        dproj = dproj + lax.dot_general(
            back,
            picks[step].astype(jnp.float32),
            (((1,), (1,)), ((), ())),
            precision=lax.Precision.HIGHEST,
            preferred_element_type=jnp.float32,
        )
    for step, by in enumerate((1, -1)):
        block = table_gradient[:, rows + (step + 2) * ghost : rows + (step + 3) * ghost]
        back = passed_along(block, "brick", -by)
        dproj = dproj + lax.dot_general(
            back,
            picks[step + 2].astype(jnp.float32),
            (((1,), (1,)), ((), ())),
            precision=lax.Precision.HIGHEST,
            preferred_element_type=jnp.float32,
        )
    dpre = (dproj * silu_grad(pre)).astype(jnp.bfloat16)
    down_weight_gradient = lax.dot_general(
        embed, dpre, (((0,), (1,)), ((), ())), preferred_element_type=jnp.float32
    )
    down_term = lax.dot_general(
        dpre, down_weight, (((0,), (1,)), ((), ())), preferred_element_type=jnp.float32
    )
    edge_embedding_gradient = (res_term + down_term).astype(jnp.bfloat16)
    reduced_total = lax.psum(
        (residual_weight_gradient, down_weight_gradient, up_weight_gradient, basis_weight_gradient),
        ("slab", "brick"),
    )
    return (
        edge_embedding_gradient,
        reduced_total[0],
        reduced_total[1],
        reduced_total[2],
        reduced_total[3],
    )


def solution(mesh):
    in_specs = (
        P(("slab", "brick"), None),
        P(("slab", "brick"), None),
        P(None, None, ("slab", "brick")),
        P(None, ("slab", "brick")),
        P(("slab", "brick")),
        P(None, ("slab", "brick")),
        P(),
        P(),
        P(),
        P(),
    )
    out_specs = (P(("slab", "brick"), None), P(), P(), P(), P())
    return jax.shard_map(shards, mesh=mesh, in_specs=in_specs, out_specs=out_specs, check_vma=False)
```

profile of v0, /device:TPU:2, one launch (start us, length us, event | category | flops | bytes accessed | tf_op | source)
XLA Modules:
  0.0 442.0 jit_solution(11072315548361697162)
XLA Ops:
  16.3 6.4 %collective-permute-start.3 = (bf16[64,128]{1,0:T(8,128)(2,1)S(1)}, bf16[64,128]{1,0:T(8,128)(2,1)S(1)}, u32[]{:S(2)}, u32[]{:S(2)}) collective-permute-start(bf16[64,128]{1,0:T(8,128)(2,1)S(1)} %convolution_convert_fusion), channel_id=1, source_target_pairs={{0,31},{1,0},{2,1},{3,2},{4,3},{5,4},{6,5},{7,6},{8,7},{9,8},{10,9... | collective-permute-start | bytes 49160 | tf_op jit(solution)/shard_map/ppermute | solution.py:10
  25.9 30.5 %while.21 = (s32[]{:T(128)}, bf16[16,64,1024]{2,1,0:T(8,128)(2,1)S(1)}, s32[16,1024]{1,0:T(8,128)}, bf16[64,1536]{1,0:T(8,128)(2,1)S(1)}, s32[]{:T(128)}) while((s32[]{:T(128)}, bf16[16,64,1024]{2,1,0:T(8,128)(2,1)S(1)}, s32[16,1024]{1,0:T(8,128)}, bf16[64,1536]{1,0:T(8,128)(2,1)S(1)}, s32[]{:T(128)}) %tuple.49), condition=%wide.region_1.2_spmd, body=%wide.region_0.1_spmd.sunk | while | flops 202964992 | bytes 340037 | solution.py:75
  59.2 2.9 fusion.15
  62.1 93.6 %while.22 = (s32[]{:T(128)}, f32[64,1536]{1,0:T(8,128)}, f32[16,64,1024]{2,1,0:T(8,128)}, s32[16,1024]{1,0:T(8,128)}, s32[]{:T(128)}, /*index=5*/s32[]{:T(128)}) while((s32[]{:T(128)}, f32[64,1536]{1,0:T(8,128)}, f32[16,64,1024]{2,1,0:T(8,128)}, s32[16,1024]{1,0:T(8,128)}, s32[]{:T(128)}, /*index=5*/s32[]{:T(128)}) %tuple.59), condition=%wide.region_4.5_spmd.clone, body=%wide.region_3.4_spmd.clone.sunk | while | flops 1209729024 | bytes 1061459 | solution.py:104
  62.9 5.0 %fusion.80 = f32[64,1536]{1,0:T(8,128)} fusion(s32[1024]{0:T(1024)S(1)} %bitcast.73, f32[64,1536]{1,0:T(8,128)} %get-tuple-element.175, f32[16,64,1024]{2,1,0:T(8,128)} %get-tuple-element.182, s32[]{:T(128)} %get-tuple-element.174, pred[]{:T(512)S(6)} %compare.3), kind=kOutput, calls=%fused_computation.10.clone.1 | convolution fusion | flops 1209729024 | bytes 1053185 | tf_op jit(solution)/shard_map/while/body/eval_jaxpr/dot_general | solution.py:95
  68.6 5.1 %fusion.80 = f32[64,1536]{1,0:T(8,128)} fusion(s32[1024]{0:T(1024)S(1)} %bitcast.73, f32[64,1536]{1,0:T(8,128)} %get-tuple-element.175, f32[16,64,1024]{2,1,0:T(8,128)} %get-tuple-element.182, s32[]{:T(128)} %get-tuple-element.174, pred[]{:T(512)S(6)} %compare.3), kind=kOutput, calls=%fused_computation.10.clone.1 | convolution fusion | flops 1209729024 | bytes 1053185 | tf_op jit(solution)/shard_map/while/body/eval_jaxpr/dot_general | solution.py:95
  74.5 5.1 %fusion.80 = f32[64,1536]{1,0:T(8,128)} fusion(s32[1024]{0:T(1024)S(1)} %bitcast.73, f32[64,1536]{1,0:T(8,128)} %get-tuple-element.175, f32[16,64,1024]{2,1,0:T(8,128)} %get-tuple-element.182, s32[]{:T(128)} %get-tuple-element.174, pred[]{:T(512)S(6)} %compare.3), kind=kOutput, calls=%fused_computation.10.clone.1 | convolution fusion | flops 1209729024 | bytes 1053185 | tf_op jit(solution)/shard_map/while/body/eval_jaxpr/dot_general | solution.py:95
  80.4 5.1 %fusion.80 = f32[64,1536]{1,0:T(8,128)} fusion(s32[1024]{0:T(1024)S(1)} %bitcast.73, f32[64,1536]{1,0:T(8,128)} %get-tuple-element.175, f32[16,64,1024]{2,1,0:T(8,128)} %get-tuple-element.182, s32[]{:T(128)} %get-tuple-element.174, pred[]{:T(512)S(6)} %compare.3), kind=kOutput, calls=%fused_computation.10.clone.1 | convolution fusion | flops 1209729024 | bytes 1053185 | tf_op jit(solution)/shard_map/while/body/eval_jaxpr/dot_general | solution.py:95
  86.2 5.1 %fusion.80 = f32[64,1536]{1,0:T(8,128)} fusion(s32[1024]{0:T(1024)S(1)} %bitcast.73, f32[64,1536]{1,0:T(8,128)} %get-tuple-element.175, f32[16,64,1024]{2,1,0:T(8,128)} %get-tuple-element.182, s32[]{:T(128)} %get-tuple-element.174, pred[]{:T(512)S(6)} %compare.3), kind=kOutput, calls=%fused_computation.10.clone.1 | convolution fusion | flops 1209729024 | bytes 1053185 | tf_op jit(solution)/shard_map/while/body/eval_jaxpr/dot_general | solution.py:95
  92.1 5.1 %fusion.80 = f32[64,1536]{1,0:T(8,128)} fusion(s32[1024]{0:T(1024)S(1)} %bitcast.73, f32[64,1536]{1,0:T(8,128)} %get-tuple-element.175, f32[16,64,1024]{2,1,0:T(8,128)} %get-tuple-element.182, s32[]{:T(128)} %get-tuple-element.174, pred[]{:T(512)S(6)} %compare.3), kind=kOutput, calls=%fused_computation.10.clone.1 | convolution fusion | flops 1209729024 | bytes 1053185 | tf_op jit(solution)/shard_map/while/body/eval_jaxpr/dot_general | solution.py:95
  97.9 5.1 %fusion.80 = f32[64,1536]{1,0:T(8,128)} fusion(s32[1024]{0:T(1024)S(1)} %bitcast.73, f32[64,1536]{1,0:T(8,128)} %get-tuple-element.175, f32[16,64,1024]{2,1,0:T(8,128)} %get-tuple-element.182, s32[]{:T(128)} %get-tuple-element.174, pred[]{:T(512)S(6)} %compare.3), kind=kOutput, calls=%fused_computation.10.clone.1 | convolution fusion | flops 1209729024 | bytes 1053185 | tf_op jit(solution)/shard_map/while/body/eval_jaxpr/dot_general | solution.py:95
  103.8 5.1 %fusion.80 = f32[64,1536]{1,0:T(8,128)} fusion(s32[1024]{0:T(1024)S(1)} %bitcast.73, f32[64,1536]{1,0:T(8,128)} %get-tuple-element.175, f32[16,64,1024]{2,1,0:T(8,128)} %get-tuple-element.182, s32[]{:T(128)} %get-tuple-element.174, pred[]{:T(512)S(6)} %compare.3), kind=kOutput, calls=%fused_computation.10.clone.1 | convolution fusion | flops 1209729024 | bytes 1053185 | tf_op jit(solution)/shard_map/while/body/eval_jaxpr/dot_general | solution.py:95
  109.6 5.1 %fusion.80 = f32[64,1536]{1,0:T(8,128)} fusion(s32[1024]{0:T(1024)S(1)} %bitcast.73, f32[64,1536]{1,0:T(8,128)} %get-tuple-element.175, f32[16,64,1024]{2,1,0:T(8,128)} %get-tuple-element.182, s32[]{:T(128)} %get-tuple-element.174, pred[]{:T(512)S(6)} %compare.3), kind=kOutput, calls=%fused_computation.10.clone.1 | convolution fusion | flops 1209729024 | bytes 1053185 | tf_op jit(solution)/shard_map/while/body/eval_jaxpr/dot_general | solution.py:95
  115.5 5.1 %fusion.80 = f32[64,1536]{1,0:T(8,128)} fusion(s32[1024]{0:T(1024)S(1)} %bitcast.73, f32[64,1536]{1,0:T(8,128)} %get-tuple-element.175, f32[16,64,1024]{2,1,0:T(8,128)} %get-tuple-element.182, s32[]{:T(128)} %get-tuple-element.174, pred[]{:T(512)S(6)} %compare.3), kind=kOutput, calls=%fused_computation.10.clone.1 | convolution fusion | flops 1209729024 | bytes 1053185 | tf_op jit(solution)/shard_map/while/body/eval_jaxpr/dot_general | solution.py:95
  121.4 5.1 %fusion.80 = f32[64,1536]{1,0:T(8,128)} fusion(s32[1024]{0:T(1024)S(1)} %bitcast.73, f32[64,1536]{1,0:T(8,128)} %get-tuple-element.175, f32[16,64,1024]{2,1,0:T(8,128)} %get-tuple-element.182, s32[]{:T(128)} %get-tuple-element.174, pred[]{:T(512)S(6)} %compare.3), kind=kOutput, calls=%fused_computation.10.clone.1 | convolution fusion | flops 1209729024 | bytes 1053185 | tf_op jit(solution)/shard_map/while/body/eval_jaxpr/dot_general | solution.py:95
  127.2 5.1 %fusion.80 = f32[64,1536]{1,0:T(8,128)} fusion(s32[1024]{0:T(1024)S(1)} %bitcast.73, f32[64,1536]{1,0:T(8,128)} %get-tuple-element.175, f32[16,64,1024]{2,1,0:T(8,128)} %get-tuple-element.182, s32[]{:T(128)} %get-tuple-element.174, pred[]{:T(512)S(6)} %compare.3), kind=kOutput, calls=%fused_computation.10.clone.1 | convolution fusion | flops 1209729024 | bytes 1053185 | tf_op jit(solution)/shard_map/while/body/eval_jaxpr/dot_general | solution.py:95
  133.1 5.1 %fusion.80 = f32[64,1536]{1,0:T(8,128)} fusion(s32[1024]{0:T(1024)S(1)} %bitcast.73, f32[64,1536]{1,0:T(8,128)} %get-tuple-element.175, f32[16,64,1024]{2,1,0:T(8,128)} %get-tuple-element.182, s32[]{:T(128)} %get-tuple-element.174, pred[]{:T(512)S(6)} %compare.3), kind=kOutput, calls=%fused_computation.10.clone.1 | convolution fusion | flops 1209729024 | bytes 1053185 | tf_op jit(solution)/shard_map/while/body/eval_jaxpr/dot_general | solution.py:95
  138.9 5.1 %fusion.80 = f32[64,1536]{1,0:T(8,128)} fusion(s32[1024]{0:T(1024)S(1)} %bitcast.73, f32[64,1536]{1,0:T(8,128)} %get-tuple-element.175, f32[16,64,1024]{2,1,0:T(8,128)} %get-tuple-element.182, s32[]{:T(128)} %get-tuple-element.174, pred[]{:T(512)S(6)} %compare.3), kind=kOutput, calls=%fused_computation.10.clone.1 | convolution fusion | flops 1209729024 | bytes 1053185 | tf_op jit(solution)/shard_map/while/body/eval_jaxpr/dot_general | solution.py:95
  144.8 5.1 %fusion.80 = f32[64,1536]{1,0:T(8,128)} fusion(s32[1024]{0:T(1024)S(1)} %bitcast.73, f32[64,1536]{1,0:T(8,128)} %get-tuple-element.175, f32[16,64,1024]{2,1,0:T(8,128)} %get-tuple-element.182, s32[]{:T(128)} %get-tuple-element.174, pred[]{:T(512)S(6)} %compare.3), kind=kOutput, calls=%fused_computation.10.clone.1 | convolution fusion | flops 1209729024 | bytes 1053185 | tf_op jit(solution)/shard_map/while/body/eval_jaxpr/dot_general | solution.py:95
  150.7 5.1 %fusion.80 = f32[64,1536]{1,0:T(8,128)} fusion(s32[1024]{0:T(1024)S(1)} %bitcast.73, f32[64,1536]{1,0:T(8,128)} %get-tuple-element.175, f32[16,64,1024]{2,1,0:T(8,128)} %get-tuple-element.182, s32[]{:T(128)} %get-tuple-element.174, pred[]{:T(512)S(6)} %compare.3), kind=kOutput, calls=%fused_computation.10.clone.1 | convolution fusion | flops 1209729024 | bytes 1053185 | tf_op jit(solution)/shard_map/while/body/eval_jaxpr/dot_general | solution.py:95
  156.6 3.7 collective-permute-start.6
  162.5 4.1 collective-permute-start.4
  173.2 76.4 %psum.31 = f32[16,64]{1,0:T(8,128)} all-reduce(f32[16,64]{1,0:T(8,128)S(1)} %fusion.25), channel_id=1, replica_groups=mesh['slab'=8,'brick'=32] {'slab','brick'}, use_global_device_ids=true, to_apply=%region_8.9 | all-reduce | flops 1024 | bytes 8192 | tf_op jit(solution)/shard_map/psum | solution.py:138
  251.8 179.5 %all-reduce.3.cloned.1.call-done = (f32[512,512]{0,1:T(8,128)}, f32[512,64]{0,1:T(8,128)}, f32[64,512]{1,0:T(8,128)}) async-done(((f32[512,512]{0,1:T(8,128)}, f32[512,64]{0,1:T(8,128)}, f32[64,512]{1,0:T(8,128)}), (f32[512,512]{0,1:T(8,128)}, f32[512,64]{0,1:T(8,128)}, f32[64,512]{1,0:T(8,128)})) %all-reduce.3.cloned.1.call-update) | async-done | bytes 1310736 | tf_op jit(solution)/shard_map/psum | solution.py:138
  (125 shorter events, 73.1 us)
Async XLA Ops:
  7.2 15.5 %copy-start.12 = (bf16[1024,512]{1,0:T(8,128)(2,1)S(1)}, bf16[1024,512]{1,0:T(8,128)(2,1)}, u32[]{:S(2)}) copy-start(bf16[1024,512]{1,0:T(8,128)(2,1)} %param.15) | copy-start | bytes 3145732
  7.2 15.5 %copy-start.3 = (bf16[512,512]{1,0:T(8,128)(2,1)S(1)}, bf16[512,512]{1,0:T(8,128)(2,1)}, u32[]{:S(2)}) copy-start(bf16[512,512]{1,0:T(8,128)(2,1)} %param.20) | copy-start | bytes 1572868
  7.2 424.1 %all-reduce.3.cloned.1.call-start = ((), (), s32[]{:S(2)}) async-start(), calls=%async_computation | async-start | bytes 2621440 | tf_op jit(solution)/shard_map/psum | solution.py:138
  11.3 14.5 %collective-permute-start = (bf16[64,128]{1,0:T(8,128)(2,1)}, bf16[64,128]{1,0:T(8,128)(2,1)S(1)}, u32[]{:S(2)}, u32[]{:S(2)}) collective-permute-start(bf16[64,128]{1,0:T(8,128)(2,1)} %convolution_convert_fusion.3), channel_id=1, source_target_pairs={{0,32},{32,64},{64,96},{96,128},{128,160},{160,192},{192,224},{224... | collective-permute-start | bytes 49160 | tf_op jit(solution)/shard_map/ppermute | solution.py:10
  13.1 12.7 %collective-permute-start.1 = (bf16[64,128]{1,0:T(8,128)(2,1)S(1)}, bf16[64,128]{1,0:T(8,128)(2,1)S(1)}, u32[]{:S(2)}, u32[]{:S(2)}) collective-permute-start(bf16[64,128]{1,0:T(8,128)(2,1)S(1)} %convolution_convert_fusion.2), channel_id=1, source_target_pairs={{0,224},{32,0},{64,32},{96,64},{128,96},{160,128},{192,160},{224,1... | collective-permute-start | bytes 49160 | tf_op jit(solution)/shard_map/ppermute | solution.py:10
  16.0 9.9 %collective-permute-start.2 = (bf16[64,128]{1,0:T(8,128)(2,1)S(1)}, bf16[64,128]{1,0:T(8,128)(2,1)S(1)}, u32[]{:S(2)}, u32[]{:S(2)}) collective-permute-start(bf16[64,128]{1,0:T(8,128)(2,1)S(1)} %convolution_convert_fusion.1), channel_id=1, source_target_pairs={{0,1},{1,2},{2,3},{3,4},{4,5},{5,6},{6,7},{7,8},{8,9},{9,10},{10,1... | collective-permute-start | bytes 49160 | tf_op jit(solution)/shard_map/ppermute | solution.py:10
  16.3 9.5 %collective-permute-start.3 = (bf16[64,128]{1,0:T(8,128)(2,1)S(1)}, bf16[64,128]{1,0:T(8,128)(2,1)S(1)}, u32[]{:S(2)}, u32[]{:S(2)}) collective-permute-start(bf16[64,128]{1,0:T(8,128)(2,1)S(1)} %convolution_convert_fusion), channel_id=1, source_target_pairs={{0,31},{1,0},{2,1},{3,2},{4,3},{5,4},{6,5},{7,6},{8,7},{9,8},{10,9... | collective-permute-start | bytes 49160 | tf_op jit(solution)/shard_map/ppermute | solution.py:10
  24.0 1.8 copy-start.1
  24.0 1.8 copy-start.11
  25.9 30.5 %copy-start.10 = (bf16[16,64]{1,0:T(8,128)(2,1)S(1)}, bf16[16,64]{1,0:T(8,128)(2,1)}, u32[]{:S(2)}) copy-start(bf16[16,64]{1,0:T(8,128)(2,1)} %param.23) | copy-start | bytes 6148
  56.4 2.3 copy-start.13
  56.4 2.3 copy-start.14
  59.2 2.9 copy-start.5
  155.7 14.1 %copy-start.9 = (f32[64,1536]{1,0:T(8,128)S(1)}, f32[64,1536]{1,0:T(8,128)}, u32[]{:S(2)}) copy-start(f32[64,1536]{1,0:T(8,128)} %get-tuple-element.50) | copy-start | bytes 1179652
  155.8 14.1 %copy-start.15 = (f32[64,1024]{1,0:T(8,128)S(1)}, f32[64,1024]{1,0:T(8,128)}, u32[]{:S(2)}) copy-start(f32[64,1024]{1,0:T(8,128)} %get-tuple-element.100) | copy-start | bytes 786436
  156.6 10.0 %collective-permute-start.6 = (f32[64,128]{1,0:T(8,128)S(1)}, f32[64,128]{1,0:T(8,128)S(1)}, u32[]{:S(2)}, u32[]{:S(2)}) collective-permute-start(f32[64,128]{1,0:T(8,128)S(1)} %get-tuple-element.95), channel_id=1, source_target_pairs={{0,31},{1,0},{2,1},{3,2},{4,3},{5,4},{6,5},{7,6},{8,7},{9,8},{10,9... | collective-permute-start | bytes 98312 | tf_op jit(solution)/shard_map/ppermute | solution.py:10
  162.5 6.0 %collective-permute-start.5 = (f32[64,128]{1,0:T(8,128)S(1)}, f32[64,128]{1,0:T(8,128)S(1)}, u32[]{:S(2)}, u32[]{:S(2)}) collective-permute-start(f32[64,128]{1,0:T(8,128)S(1)} %get-tuple-element.93), channel_id=1, source_target_pairs={{0,32},{32,64},{64,96},{96,128},{128,160},{160,192},{192,224},{224... | collective-permute-start | bytes 98312 | tf_op jit(solution)/shard_map/ppermute | solution.py:10
  162.5 7.0 %collective-permute-start.7 = (f32[64,128]{1,0:T(8,128)S(1)}, f32[64,128]{1,0:T(8,128)S(1)}, u32[]{:S(2)}, u32[]{:S(2)}) collective-permute-start(f32[64,128]{1,0:T(8,128)S(1)} %get-tuple-element.94), channel_id=1, source_target_pairs={{0,1},{1,2},{2,3},{3,4},{4,5},{5,6},{6,7},{7,8},{8,9},{9,10},{10,1... | collective-permute-start | bytes 98312 | tf_op jit(solution)/shard_map/ppermute | solution.py:10
  162.5 7.4 %collective-permute-start.4 = (f32[64,128]{1,0:T(8,128)S(1)}, f32[64,128]{1,0:T(8,128)S(1)}, u32[]{:S(2)}, u32[]{:S(2)}) collective-permute-start(f32[64,128]{1,0:T(8,128)S(1)} %get-tuple-element.92), channel_id=1, source_target_pairs={{0,224},{32,0},{64,32},{96,64},{128,96},{160,128},{192,160},{224,1... | collective-permute-start | bytes 98312 | tf_op jit(solution)/shard_map/ppermute | solution.py:10
  171.3 78.2 %copy-start.8 = (bf16[512,64]{0,1:T(8,128)(2,1)S(1)}, bf16[512,64]{0,1:T(8,128)(2,1)}, u32[]{:S(2)}) copy-start(bf16[512,64]{0,1:T(8,128)(2,1)} %param.21) | copy-start | bytes 196612
  173.2 76.9 %copy-start.2 = (bf16[1024,512]{1,0:T(8,128)(2,1)S(1)}, bf16[1024,512]{1,0:T(8,128)(2,1)}, u32[]{:S(2)}) copy-start(bf16[1024,512]{1,0:T(8,128)(2,1)} %copy-done.1) | copy-start | bytes 3145732
  173.2 76.9 %copy-start.4 = (bf16[512,512]{1,0:T(8,128)(2,1)S(1)}, bf16[512,512]{1,0:T(8,128)(2,1)}, u32[]{:S(2)}) copy-start(bf16[512,512]{1,0:T(8,128)(2,1)} %param.20) | copy-start | bytes 1572868
  431.3 2.6 copy-start.7
  431.3 3.2 copy-start.6
  (1 other events, 1.3 us)
Sparse Core Ops, SparseCore 0:
  171.5 259.7 all-reduce.2
where the time goes:
time: 445 us; the launch traced here: 442 us
  waiting for transfers between devices  182 us (41%)
  matrix products  117 us (26%)
  blocking collectives  76.4 us (17%)
  local copies, waits for them, and re-layouts  30.6 us (7%)
  starting transfers between devices  18.5 us (4%)
  between operations  14.3 us (3%)
    psum x1, waiting for transfers between devices, shards(): lax.psum((residual_weight_gradient, down_weight_gradient, up_weight_gradi...  179 us
    dot_general x16, matrix products, scatter_slot(): lax.dot_general(slot_terms, onehot, (((1,), (1,)), ((), ())), precision=l...  81.4 us
    psum x1, blocking collectives, shards(): lax.psum((residual_weight_gradient, down_weight_gradient, up_weight_gradi...  76.4 us
    dynamic_slice x32, local copies, waits for them, and re-layouts, shards(): lax.scan(gather_slot, jnp.zeros((), jnp.float32), triplet_row_index)  24.5 us
    ppermute x8, starting transfers between devices, passed_along(): return lax.ppermute(value, axis, pairs)  18.5 us
    dot_general x16, matrix products, gather_slot(): jnp.dot(edge_table_rows, onehot, preferred_element_type=jnp.float32)  18 us
  transfers between devices with their start and end apart: 9, of which 3 were waited for; matrix products, arithmetic and copies ran while one was open for 3% of the time, Pallas kernels for 0%

commit v1 on v0

--- a/solution.py
+++ b/solution.py
@@ -136,8 +136,16 @@
     )
     edge_embedding_gradient = (res_term + down_term).astype(jnp.bfloat16)
     reduced_total = lax.psum(
-        (residual_weight_gradient, down_weight_gradient, up_weight_gradient, basis_weight_gradient),
-        ("slab", "brick"),
+        lax.psum(
+            (
+                residual_weight_gradient,
+                down_weight_gradient,
+                up_weight_gradient,
+                basis_weight_gradient,
+            ),
+            "slab",
+        ),
+        "brick",
     )
     return (
         edge_embedding_gradient,

time: 445 us -> 541 us (1.22)
  waiting for transfers between devices: 182 us -> 267 us
  blocking collectives: 76.4 us -> 85 us
    psum x0 -> x1, waiting for transfers between devices: none -> 185 us  [shards(): lax.psum(lax.psum((residual_weight_gradient, down_weight_gradient, up_wei...]
    psum x1, waiting for transfers between devices: 179 us -> 80.5 us  [shards(): lax.psum((residual_weight_gradient, down_weight_gradient, up_weight_gradi...]
    psum x0 -> x1, blocking collectives: none -> 66.7 us  [shards(): lax.psum(lax.psum((residual_weight_gradient, down_weight_gradient, up_wei...]
    psum x1, blocking collectives: 76.4 us -> 18.3 us  [shards(): lax.psum((residual_weight_gradient, down_weight_gradient, up_weight_gradi...]
  transfers between devices with their start and end apart: 9 -> 10, of which waited for: 3 -> 4; matrix products, arithmetic and copies ran while one was open for 3% -> 2% of each run, Pallas kernels for 0% -> 0%
where the time goes in v1:
time: 541 us; the launch traced here: 536 us
  waiting for transfers between devices  267 us (49%)
  matrix products  117 us (22%)
  blocking collectives  85 us (16%)
  local copies, waits for them, and re-layouts  30.6 us (6%)
  starting transfers between devices  18.6 us (3%)
  between operations  14.3 us (3%)
    psum x1, waiting for transfers between devices, shards(): lax.psum(lax.psum((residual_weight_gradient, down_weight_gradient, up_wei...  185 us
    dot_general x16, matrix products, scatter_slot(): lax.dot_general(slot_terms, onehot, (((1,), (1,)), ((), ())), precision=l...  81.4 us
    psum x1, waiting for transfers between devices, shards(): lax.psum((residual_weight_gradient, down_weight_gradient, up_weight_gradi...  80.5 us
    psum x1, blocking collectives, shards(): lax.psum(lax.psum((residual_weight_gradient, down_weight_gradient, up_wei...  66.7 us
    dynamic_slice x32, local copies, waits for them, and re-layouts, shards(): lax.scan(gather_slot, jnp.zeros((), jnp.float32), triplet_row_index)  24.5 us
    ppermute x8, starting transfers between devices, passed_along(): return lax.ppermute(value, axis, pairs)  18.5 us
    psum x1, blocking collectives, shards(): lax.psum((residual_weight_gradient, down_weight_gradient, up_weight_gradi...  18.3 us
    dot_general x16, matrix products, gather_slot(): jnp.dot(edge_table_rows, onehot, preferred_element_type=jnp.float32)  18 us
  transfers between devices with their start and end apart: 10, of which 4 were waited for; matrix products, arithmetic and copies ran while one was open for 2% of the time, Pallas kernels for 0%

profile of v1, /device:TPU:2, one launch (start us, length us, event | category | flops | bytes accessed | tf_op | source)
XLA Modules:
  0.0 536.3 jit_solution(492509099226611664)
XLA Ops:
  16.3 6.4 %collective-permute-start.3 = (bf16[64,128]{1,0:T(8,128)(2,1)S(1)}, bf16[64,128]{1,0:T(8,128)(2,1)S(1)}, u32[]{:S(2)}, u32[]{:S(2)}) collective-permute-start(bf16[64,128]{1,0:T(8,128)(2,1)S(1)} %convolution_convert_fusion), channel_id=1, source_target_pairs={{0,31},{1,0},{2,1},{3,2},{4,3},{5,4},{6,5},{7,6},{8,7},{9,8},{10,9... | collective-permute-start | bytes 49160 | tf_op jit(solution)/shard_map/ppermute | solution.py:10
  25.9 30.5 %while.21 = (s32[]{:T(128)}, bf16[16,64,1024]{2,1,0:T(8,128)(2,1)S(1)}, s32[16,1024]{1,0:T(8,128)}, bf16[64,1536]{1,0:T(8,128)(2,1)S(1)}, s32[]{:T(128)}) while((s32[]{:T(128)}, bf16[16,64,1024]{2,1,0:T(8,128)(2,1)S(1)}, s32[16,1024]{1,0:T(8,128)}, bf16[64,1536]{1,0:T(8,128)(2,1)S(1)}, s32[]{:T(128)}) %tuple.49), condition=%wide.region_1.2_spmd, body=%wide.region_0.1_spmd.sunk | while | flops 202964992 | bytes 340037 | solution.py:75
  62.1 93.6 %while.22 = (s32[]{:T(128)}, f32[64,1536]{1,0:T(8,128)}, f32[16,64,1024]{2,1,0:T(8,128)}, s32[16,1024]{1,0:T(8,128)}, s32[]{:T(128)}, /*index=5*/s32[]{:T(128)}) while((s32[]{:T(128)}, f32[64,1536]{1,0:T(8,128)}, f32[16,64,1024]{2,1,0:T(8,128)}, s32[16,1024]{1,0:T(8,128)}, s32[]{:T(128)}, /*index=5*/s32[]{:T(128)}) %tuple.62), condition=%wide.region_4.5_spmd.clone, body=%wide.region_3.4_spmd.clone.sunk | while | flops 1209729024 | bytes 1061459 | solution.py:104
  62.9 5.0 fusion.80
  68.6 5.1 fusion.80
  74.5 5.1 fusion.80
  80.3 5.1 fusion.80
  86.2 5.1 fusion.80
  92.0 5.1 fusion.80
  97.9 5.1 fusion.80
  103.8 5.1 fusion.80
  109.6 5.1 fusion.80
  115.5 5.1 fusion.80
  121.3 5.1 fusion.80
  127.2 5.1 fusion.80
  133.0 5.1 fusion.80
  138.9 5.1 fusion.80
  144.8 5.1 fusion.80
  150.6 5.1 fusion.80
  162.5 4.1 collective-permute-start.4
  171.4 80.5 %all-reduce.7.cloned.1.call-done = (f32[512,512]{0,1:T(8,128)}, f32[512,64]{0,1:T(8,128)}, f32[64,512]{1,0:T(8,128)}) async-done(((f32[512,512]{0,1:T(8,128)}, f32[512,64]{0,1:T(8,128)}, f32[64,512]{1,0:T(8,128)}), (f32[512,512]{0,1:T(8,128)}, f32[512,64]{0,1:T(8,128)}, f32[64,512]{1,0:T(8,128)})) %all-reduce.7.cloned.1.call-update) | async-done | bytes 1310736 | tf_op jit(solution)/shard_map/psum | solution.py:139
  253.7 18.3 %psum.62 = f32[16,64]{1,0:T(8,128)S(1)} all-reduce(f32[16,64]{1,0:T(8,128)S(1)} %fusion.25), channel_id=1, replica_groups=mesh['slab'=8,'brick'=32] {'slab'}, use_global_device_ids=true, to_apply=%region_11.12 | all-reduce | flops 1024 | bytes 8192 | tf_op jit(solution)/shard_map/psum | solution.py:139
  272.0 66.7 %psum.63 = f32[16,64]{1,0:T(8,128)} all-reduce(f32[16,64]{1,0:T(8,128)S(1)} %psum.62), channel_id=1, replica_groups=mesh['slab'=8,'brick'=32] {'brick'}, use_global_device_ids=true, to_apply=%region_12.13 | all-reduce | flops 1024 | bytes 8192 | tf_op jit(solution)/shard_map/psum | solution.py:138
  340.9 184.7 %all-reduce.5.cloned.1.call-done = (f32[512,512]{0,1:T(8,128)}, f32[512,64]{0,1:T(8,128)}, f32[64,512]{1,0:T(8,128)}) async-done(((f32[512,512]{0,1:T(8,128)}, f32[512,64]{0,1:T(8,128)}, f32[64,512]{1,0:T(8,128)}), (f32[512,512]{0,1:T(8,128)}, f32[512,64]{0,1:T(8,128)}, f32[64,512]{1,0:T(8,128)})) %all-reduce.5.cloned.1.call-update) | async-done | bytes 1310736 | tf_op jit(solution)/shard_map/psum | solution.py:138
  (129 shorter events, 79.7 us)
Async XLA Ops:
  7.2 15.5 %copy-start.12 = (bf16[1024,512]{1,0:T(8,128)(2,1)S(1)}, bf16[1024,512]{1,0:T(8,128)(2,1)}, u32[]{:S(2)}) copy-start(bf16[1024,512]{1,0:T(8,128)(2,1)} %param.15) | copy-start | bytes 3145732
  7.2 15.5 %copy-start.3 = (bf16[512,512]{1,0:T(8,128)(2,1)S(1)}, bf16[512,512]{1,0:T(8,128)(2,1)}, u32[]{:S(2)}) copy-start(bf16[512,512]{1,0:T(8,128)(2,1)} %param.20) | copy-start | bytes 1572868
  7.2 244.6 %all-reduce.7.cloned.1.call-start = ((), (), s32[]{:S(2)}) async-start(), calls=%async_computation.1 | async-start | bytes 2621440 | tf_op jit(solution)/shard_map/psum | solution.py:139
  11.3 14.5 %collective-permute-start = (bf16[64,128]{1,0:T(8,128)(2,1)}, bf16[64,128]{1,0:T(8,128)(2,1)S(1)}, u32[]{:S(2)}, u32[]{:S(2)}) collective-permute-start(bf16[64,128]{1,0:T(8,128)(2,1)} %convolution_convert_fusion.3), channel_id=1, source_target_pairs={{0,32},{32,64},{64,96},{96,128},{128,160},{160,192},{192,224},{224... | collective-permute-start | bytes 49160 | tf_op jit(solution)/shard_map/ppermute | solution.py:10
  13.1 12.7 %collective-permute-start.1 = (bf16[64,128]{1,0:T(8,128)(2,1)S(1)}, bf16[64,128]{1,0:T(8,128)(2,1)S(1)}, u32[]{:S(2)}, u32[]{:S(2)}) collective-permute-start(bf16[64,128]{1,0:T(8,128)(2,1)S(1)} %convolution_convert_fusion.2), channel_id=1, source_target_pairs={{0,224},{32,0},{64,32},{96,64},{128,96},{160,128},{192,160},{224,1... | collective-permute-start | bytes 49160 | tf_op jit(solution)/shard_map/ppermute | solution.py:10
  16.0 9.8 %collective-permute-start.2 = (bf16[64,128]{1,0:T(8,128)(2,1)S(1)}, bf16[64,128]{1,0:T(8,128)(2,1)S(1)}, u32[]{:S(2)}, u32[]{:S(2)}) collective-permute-start(bf16[64,128]{1,0:T(8,128)(2,1)S(1)} %convolution_convert_fusion.1), channel_id=1, source_target_pairs={{0,1},{1,2},{2,3},{3,4},{4,5},{5,6},{6,7},{7,8},{8,9},{9,10},{10,1... | collective-permute-start | bytes 49160 | tf_op jit(solution)/shard_map/ppermute | solution.py:10
  16.3 9.5 %collective-permute-start.3 = (bf16[64,128]{1,0:T(8,128)(2,1)S(1)}, bf16[64,128]{1,0:T(8,128)(2,1)S(1)}, u32[]{:S(2)}, u32[]{:S(2)}) collective-permute-start(bf16[64,128]{1,0:T(8,128)(2,1)S(1)} %convolution_convert_fusion), channel_id=1, source_target_pairs={{0,31},{1,0},{2,1},{3,2},{4,3},{5,4},{6,5},{7,6},{8,7},{9,8},{10,9... | collective-permute-start | bytes 49160 | tf_op jit(solution)/shard_map/ppermute | solution.py:10
  24.0 1.7 copy-start.1
  25.9 30.5 %copy-start.10 = (bf16[16,64]{1,0:T(8,128)(2,1)S(1)}, bf16[16,64]{1,0:T(8,128)(2,1)}, u32[]{:S(2)}) copy-start(bf16[16,64]{1,0:T(8,128)(2,1)} %param.23) | copy-start | bytes 6148
  56.4 2.3 copy-start.13
  56.4 2.3 copy-start.14
  59.2 2.9 copy-start.5
  155.7 14.1 %copy-start.9 = (f32[64,1536]{1,0:T(8,128)S(1)}, f32[64,1536]{1,0:T(8,128)}, u32[]{:S(2)}) copy-start(f32[64,1536]{1,0:T(8,128)} %get-tuple-element.50) | copy-start | bytes 1179652
  155.7 14.1 %copy-start.15 = (f32[64,1024]{1,0:T(8,128)S(1)}, f32[64,1024]{1,0:T(8,128)}, u32[]{:S(2)}) copy-start(f32[64,1024]{1,0:T(8,128)} %get-tuple-element.103) | copy-start | bytes 786436
  156.6 10.0 %collective-permute-start.6 = (f32[64,128]{1,0:T(8,128)S(1)}, f32[64,128]{1,0:T(8,128)S(1)}, u32[]{:S(2)}, u32[]{:S(2)}) collective-permute-start(f32[64,128]{1,0:T(8,128)S(1)} %get-tuple-element.98), channel_id=1, source_target_pairs={{0,31},{1,0},{2,1},{3,2},{4,3},{5,4},{6,5},{7,6},{8,7},{9,8},{10,9... | collective-permute-start | bytes 98312 | tf_op jit(solution)/shard_map/ppermute | solution.py:10
  162.5 6.0 %collective-permute-start.5 = (f32[64,128]{1,0:T(8,128)S(1)}, f32[64,128]{1,0:T(8,128)S(1)}, u32[]{:S(2)}, u32[]{:S(2)}) collective-permute-start(f32[64,128]{1,0:T(8,128)S(1)} %get-tuple-element.96), channel_id=1, source_target_pairs={{0,32},{32,64},{64,96},{96,128},{128,160},{160,192},{192,224},{224... | collective-permute-start | bytes 98312 | tf_op jit(solution)/shard_map/ppermute | solution.py:10
  162.5 7.0 %collective-permute-start.7 = (f32[64,128]{1,0:T(8,128)S(1)}, f32[64,128]{1,0:T(8,128)S(1)}, u32[]{:S(2)}, u32[]{:S(2)}) collective-permute-start(f32[64,128]{1,0:T(8,128)S(1)} %get-tuple-element.97), channel_id=1, source_target_pairs={{0,1},{1,2},{2,3},{3,4},{4,5},{5,6},{6,7},{7,8},{8,9},{9,10},{10,1... | collective-permute-start | bytes 98312 | tf_op jit(solution)/shard_map/ppermute | solution.py:10
  162.5 7.4 %collective-permute-start.4 = (f32[64,128]{1,0:T(8,128)S(1)}, f32[64,128]{1,0:T(8,128)S(1)}, u32[]{:S(2)}, u32[]{:S(2)}) collective-permute-start(f32[64,128]{1,0:T(8,128)S(1)} %get-tuple-element.95), channel_id=1, source_target_pairs={{0,224},{32,0},{64,32},{96,64},{128,96},{160,128},{192,160},{224,1... | collective-permute-start | bytes 98312 | tf_op jit(solution)/shard_map/ppermute | solution.py:10
  171.3 354.3 %all-reduce.5.cloned.1.call-start = ((), (), s32[]{:S(2)}) async-start(), calls=%async_computation | async-start | bytes 2621440 | tf_op jit(solution)/shard_map/psum | solution.py:138
  251.9 86.8 %copy-start.8 = (bf16[512,64]{0,1:T(8,128)(2,1)S(1)}, bf16[512,64]{0,1:T(8,128)(2,1)}, u32[]{:S(2)}) copy-start(bf16[512,64]{0,1:T(8,128)(2,1)} %param.21) | copy-start | bytes 196612
  253.7 85.5 %copy-start.2 = (bf16[1024,512]{1,0:T(8,128)(2,1)S(1)}, bf16[1024,512]{1,0:T(8,128)(2,1)}, u32[]{:S(2)}) copy-start(bf16[1024,512]{1,0:T(8,128)(2,1)} %copy-done.1) | copy-start | bytes 3145732
  253.7 85.5 %copy-start.4 = (bf16[512,512]{1,0:T(8,128)(2,1)S(1)}, bf16[512,512]{1,0:T(8,128)(2,1)}, u32[]{:S(2)}) copy-start(bf16[512,512]{1,0:T(8,128)(2,1)} %param.20) | copy-start | bytes 1572868
  525.6 2.6 copy-start.7
  525.6 3.2 copy-start.6
  (2 other events, 3.0 us)
Sparse Core Ops, SparseCore 0:
  171.5 80.3 all-reduce.6
  254.7 270.8 all-reduce.4
